TPU v7x, 512 devices: a whole 4x4x16 slice. The times are simulated.
512 devices in a mesh: kv: 4 (over x), tok: 128 (over y, z, core).
Axes of the slice: x: 4, y: 4, z: 16, core: 2. Of those that a mesh axis runs over, the one named last changes fastest.
Arguments:
- layer_input: bfloat16 [128, 512, 1536], P('tok', 'kv'), may hold values from -6 to 6
- queries: bfloat16 [128, 512, 1536], P('tok', None, 'kv'), may hold values from -80 to 80
- keys_new: bfloat16 [128, 512, 512], P('tok', None, 'kv'), may hold values from -4 to 4
- values_new: bfloat16 [128, 512, 512], P('tok', None, 'kv'), may hold values from -6 to 6
- cache_keys: bfloat16 [128, 1024, 512], P('tok', None, 'kv'), may hold values from -4 to 4
- cache_values: bfloat16 [128, 1024, 512], P('tok', None, 'kv'), may hold values from -6 to 6
- cache_length: int32 [128], P('tok'), may hold values from 128 to 1024, as said below
- cache_start: int32 [128], P('tok'), may hold values from 0 to 256, as said below
- output_proj: bfloat16 [1536, 1536], P('kv', 'tok'), may hold values from -0.15625 to 0.15625
- norm_gain: float32 [1536], replicated, may hold values from 0.1 to 1.9
- expert_routes: int32 [128, 512, 6], P('tok', 'kv'), may hold values from 0 to 63, all different within a row; in each aligned block of 128 rows (0 to 127, 128 to 255, ..., all dimensions but the last counted through in order) at most 16 rows name the same one
- route_weights: float32 [128, 512, 6], P('tok', 'kv'), may hold values from 0.05 to 0.35
- piece_gate_up: bfloat16 [128, 1536, 512], P('tok'), may hold values from -0.15625 to 0.15625
- piece_down: bfloat16 [128, 256, 1536], P('tok'), may hold values from -0.25 to 0.25
Outputs:
- layer_output: bfloat16 [128, 512, 1536], P('tok', 'kv')
Inputs may be any that keep to these rules, and one draw needn't show every extreme that they name: `cache_length`: one request in every draw has exactly 1024 cached positions. cache_start of a request is at most its cache_length // 4; one request with 1024 cached positions starts at exactly 256. `expert_routes`: the 6 experts of a token are distinct; in each aligned block of 128 tokens (the tokens of one request on one index of kv) no expert is named by more than 16 tokens, a bound that some block reaches.
All inputs are finite; a program needn't handle non-finite values.
Results may differ from a plain program's by a relative error of at most 0.0046.
Values may be sent and summed in bfloat16 or wider, within the bound.
A program may use at most 64 MiB of HBM per device.

v0:
```python
import jax
import jax.numpy as jnp
from jax import lax
from jax.sharding import PartitionSpec as P

HD = 128
EXPERTS = 64
TOPK = 6
CAP = 16


def visible_mask(length, first_visible, span_rows, cached):
    cache_pos = jnp.arange(cached, dtype=jnp.int32)
    cache_ok = jnp.logical_and(cache_pos >= first_visible, cache_pos < length)
    position = jnp.arange(span_rows, dtype=jnp.int32)
    causal = position[None, :] <= position[:, None]
    return jnp.concatenate(
        [jnp.broadcast_to(cache_ok[None, :], (span_rows, cached)), causal], axis=1
    )


def attend_heads(query_rows, all_keys, all_values, allowed):
    head_count = query_rows.shape[1] // HD
    score_scale = HD ** (-0.5)
    results = []
    for head_index in range(head_count):
        query_block = query_rows[:, head_index * HD : (head_index + 1) * HD]
        scores = jnp.dot(query_block, all_keys.T, preferred_element_type=jnp.float32) * score_scale
        scores = jnp.where(allowed, scores, -1e30)
        largest = jnp.max(scores, axis=1, keepdims=True)
        exponent = jnp.exp(scores - largest)
        attention_weights = (exponent / jnp.sum(exponent, axis=1, keepdims=True)).astype(
            jnp.bfloat16
        )
        results.append(
            jnp.dot(attention_weights, all_values, preferred_element_type=jnp.float32).astype(
                jnp.bfloat16
            )
        )
    return jnp.concatenate(results, axis=1)


def slot_places(route_rows):
    onehot = (route_rows[..., None] == jnp.arange(EXPERTS, dtype=jnp.int32)).astype(jnp.int32)
    rank_table = jnp.cumsum(onehot, axis=-2) - 1
    slot_index = jnp.sum(onehot * rank_table, axis=-1)
    return route_rows * CAP + slot_index


def run_pieces(grouped, weights_in, weights_out):
    width_half = weights_out.shape[1]
    gate_up = jnp.einsum("spcd,pdf->spcf", grouped, weights_in, preferred_element_type=jnp.float32)
    hidden = (jax.nn.silu(gate_up[..., :width_half]) * gate_up[..., width_half:]).astype(
        jnp.bfloat16
    )
    return jnp.einsum(
        "spcf,pfd->spcd", hidden, weights_out, preferred_element_type=jnp.float32
    ).astype(jnp.bfloat16)


def on_device(
    layer_input,
    queries,
    keys_new,
    values_new,
    cache_keys,
    cache_values,
    cache_length,
    cache_start,
    output_proj,
    norm_gain,
    expert_routes,
    route_weights,
    piece_gate_up,
    piece_down,
):
    span_rows = queries.shape[1]
    cached = cache_keys.shape[1]
    allowed = visible_mask(cache_length[0], cache_start[0], span_rows, cached)
    all_keys = jnp.concatenate([cache_keys[0], keys_new[0]], axis=0)
    all_values = jnp.concatenate([cache_values[0], values_new[0]], axis=0)
    attended = attend_heads(queries[0], all_keys, all_values, allowed)
    partial_sums = jnp.dot(
        attended,
        lax.all_gather(output_proj, "tok", axis=1, tiled=True),
        preferred_element_type=jnp.float32,
    )
    attention = lax.psum_scatter(partial_sums, "kv", scatter_dimension=0, tiled=True)
    residual = layer_input[0].astype(jnp.float32) + attention
    normed = (
        residual
        * lax.rsqrt(jnp.mean(residual * residual, axis=1, keepdims=True) + 1e-05)
        * norm_gain
    ).astype(jnp.bfloat16)
    block_rows = residual.shape[0]
    model_width = residual.shape[1]
    places = slot_places(expert_routes[0].reshape(block_rows * TOPK))
    slot_ids = jnp.arange(EXPERTS * CAP, dtype=jnp.int32)
    selector = jnp.any(
        places.reshape(block_rows, TOPK)[None, :, :] == slot_ids[:, None, None], axis=2
    ).astype(jnp.bfloat16)
    packed = (
        jnp.dot(selector, normed, preferred_element_type=jnp.float32)
        .astype(jnp.bfloat16)
        .reshape(EXPERTS, CAP, model_width)
    )
    owned_count = piece_gate_up.shape[0]
    outgoing = jnp.concatenate([packed, packed], axis=0)
    arrived = lax.all_to_all(outgoing, "tok", split_axis=0, concat_axis=0, tiled=True)
    sources = arrived.shape[0] // owned_count
    grouped = arrived.reshape(sources, owned_count, CAP, model_width)
    produced = run_pieces(grouped, piece_gate_up, piece_down).reshape(
        sources * owned_count, CAP, model_width
    )
    returned = lax.all_to_all(produced, "tok", split_axis=0, concat_axis=0, tiled=True)
    flat_back = returned.reshape(2 * EXPERTS * CAP, model_width)
    first_half = jnp.take(flat_back, places, axis=0)
    second_half = jnp.take(flat_back, places + EXPERTS * CAP, axis=0)
    merged = (first_half.astype(jnp.float32) + second_half.astype(jnp.float32)).reshape(
        block_rows, TOPK, model_width
    )
    routed_sum = jnp.sum(merged * route_weights[0][:, :, None], axis=1)
    return (residual + routed_sum).astype(jnp.bfloat16)[None]


def solution(mesh):
    return jax.shard_map(
        on_device,
        mesh=mesh,
        in_specs=(
            P("tok", "kv", None),
            P("tok", None, "kv"),
            P("tok", None, "kv"),
            P("tok", None, "kv"),
            P("tok", None, "kv"),
            P("tok", None, "kv"),
            P("tok"),
            P("tok"),
            P("kv", "tok"),
            P(),
            P("tok", "kv", None),
            P("tok", "kv", None),
            P("tok", None, None),
            P("tok", None, None),
        ),
        out_specs=P("tok", "kv", None),
        check_vma=False,
    )
```

profile of v0, /device:TPU:6, one launch (start us, length us, event | category | flops | bytes accessed | tf_op | source)
XLA Modules:
  0.0 845.0 jit_solution(16351048044316430844)
XLA Ops:
  6.6 0.7 all-gather.3.cloned.1.call-update
  8.7 2.6 fusion.52
  14.2 0.7 fusion.22
  14.9 0.7 fusion.21
  15.6 0.7 fusion.20
  16.3 139.1 %all-gather.3.cloned.1.call-done = bf16[128,12,384]{2,1,0:T(8,128)(2,1)} async-done(((bf16[1,12,384]{2,1,0:T(8,128)(2,1)}), bf16[128,12,384]{2,1,0:T(8,128)(2,1)}) %all-gather.3.cloned.1.call-update) | async-done | bytes 1179664 | tf_op jit(solution)/shard_map/all_gather | solution.py:85
  155.4 2.3 reshape.102
  157.7 2.7 fusion.27
  161.5 1.8 reduce-window.6
  164.5 36.4 %reduce-scatter.2.cloned.1.call-done = f32[128,1536]{1,0:T(8,128)} async-done(((f32[512,1536]{1,0:T(8,128)}), f32[128,1536]{1,0:T(8,128)}) %reduce-scatter.2.cloned.1.call-update) | async-done | bytes 786448 | tf_op jit(solution)/shard_map/reduce_scatter | solution.py:88
  200.9 1.3 multiply_reduce_fusion.1
  202.2 2.2 convolution_convert_fusion.1
  204.9 295.2 %all_to_all.10 = bf16[128,16,1536]{2,1,0:T(8,128)(2,1)S(1)} all-to-all(bf16[128,16,1536]{2,1,0:T(8,128)(2,1)S(1)} %pad_maximum_fusion), channel_id=1, replica_groups=mesh['kv'=4,'tok'=128] {'tok'}, dimensions={0} | all-to-all | bytes 12582912 | tf_op jit(solution)/shard_map/all_to_all | solution.py:109
  500.2 7.8 fusion.12
  508.0 1.9 convolution_convert_fusion
  509.9 6.4 copy.50
  516.3 9.6 %all-to-all-start.1 = ((bf16[128,16,1536]{2,1,0:T(8,128)(2,1)}), bf16[128,16,1536]{2,1,0:T(8,128)(2,1)}, u32[]{:S(2)}, u32[]{:S(2)}) async-start(bf16[128,16,1536]{2,1,0:T(8,128)(2,1)} %copy.50), calls=%async_computation.2 | async-start | bytes 12582912 | tf_op jit(solution)/shard_map/all_to_all | solution.py:115
  526.0 276.4 %all-to-all-done.1 = bf16[128,16,1536]{2,1,0:T(8,128)(2,1)} async-done(((bf16[128,16,1536]{2,1,0:T(8,128)(2,1)}), bf16[128,16,1536]{2,1,0:T(8,128)(2,1)}, u32[]{:S(2)}, u32[]{:S(2)}) %all-to-all-start.1) | async-done | bytes 6291488 | tf_op jit(solution)/shard_map/all_to_all | solution.py:115
  802.4 9.5 %gather_fusion = bf16[768,1536]{1,0:T(8,128)(2,1)} fusion(bf16[2048,1536]{1,0:T(8,128)(2,1)} %bitcast.25, s32[1024]{0:T(1024)S(1)} %get-tuple-element.19), kind=kCustom, calls=%fused_computation.clone | custom fusion | bytes 4721664 | tf_op jit(solution)/shard_map/jit(_take)/gather | solution.py:117
  811.9 9.6 %gather_fusion.1 = bf16[768,1536]{1,0:T(8,128)(2,1)} fusion(bf16[2048,1536]{1,0:T(8,128)(2,1)} %bitcast.25, s32[1024]{0:T(1024)S(1)} %get-tuple-element.18), kind=kCustom, calls=%fused_computation.1.clone | custom fusion | bytes 4721664 | tf_op jit(solution)/shard_map/jit(_take)/gather | solution.py:118
  821.5 4.3 convert_add_fusion
  825.8 6.1 reshape.81
  831.9 5.3 multiply_reduce_fusion
  837.3 0.9 fusion.26
  (54 shorter events, 5.9 us)
Async XLA Ops:
  6.5 493.7 %copy-start = (bf16[1,1536,512]{2,1,0:T(8,128)(2,1)S(1)}, bf16[1,1536,512]{2,1,0:T(8,128)(2,1)}, u32[]{:S(2)}) copy-start(bf16[1,1536,512]{2,1,0:T(8,128)(2,1)} %param.28) | copy-start | bytes 4718596
  6.5 4.8 copy-start.9
  6.5 4.8 copy-start.11
  6.5 4.8 copy-start.8
  6.5 148.9 %all-gather.3.cloned.1.call-start = ((), (), s32[]{:S(2)}) async-start(), calls=%async_computation.4 | async-start | bytes 1585152 | tf_op jit(solution)/shard_map/all_gather | solution.py:85
  7.3 193.6 %reduce-scatter.2.cloned.1.call-start = ((), (), s32[]{:S(2)}) async-start(), calls=%async_computation.3 | async-start | bytes 3932160 | tf_op jit(solution)/shard_map/reduce_scatter | solution.py:88
  13.0 1.2 copy-start.10
  13.0 1.2 copy-start.12
  160.4 0.7 copy-start.4
  160.4 40.5 %copy-start.3 = (bf16[1,128,1536]{2,1,0:T(8,128)(2,1)S(1)}, bf16[1,128,1536]{2,1,0:T(8,128)(2,1)}, u32[]{:S(2)}) copy-start(bf16[1,128,1536]{2,1,0:T(8,128)(2,1)} %param.16) | copy-start | bytes 1179652
  160.4 41.8 %copy-start.5 = (f32[1536]{0:T(1024)S(1)}, f32[1536]{0:T(1024)}, u32[]{:S(2)}) copy-start(f32[1536]{0:T(1024)} %param.25) | copy-start | bytes 18436
  500.2 7.8 copy-start.7
  516.3 9.6 %copy-start.6 = (f32[1,128,6]{1,0,2:T(1,128)S(1)}, f32[1,128,6]{1,0,2:T(1,128)}, u32[]{:S(2)}) copy-start(f32[1,128,6]{1,0,2:T(1,128)} %param.27) | copy-start | bytes 9220
  516.3 286.2 %all-to-all-start.1 = ((bf16[128,16,1536]{2,1,0:T(8,128)(2,1)}), bf16[128,16,1536]{2,1,0:T(8,128)(2,1)}, u32[]{:S(2)}, u32[]{:S(2)}) async-start(bf16[128,16,1536]{2,1,0:T(8,128)(2,1)} %copy.50), calls=%async_computation.2 | async-start | bytes 12582912 | tf_op jit(solution)/shard_map/all_to_all | solution.py:115
  831.9 6.2 copy-start.1
  831.9 5.3 copy-start.2
Sparse Core Ops, SparseCore 0:
  10.4 144.9 all-gather.2
  160.5 40.2 reduce-scatter.1
where the time goes:
time: 849 us; the launch traced here: 845 us
  waiting for transfers between devices  453 us (53%)
  blocking collectives  295 us (35%)
  local copies, waits for them, and re-layouts  35.5 us (4%)
  matrix products  20.6 us (2%)
  other arithmetic  16.5 us (2%)
  between operations  15 us (2%)
  starting transfers between devices  9.68 us (1%)
    all_to_all x1, blocking collectives, on_device(): lax.all_to_all(outgoing, 'tok', split_axis=0, concat_axis=0, tiled=True)  295 us
    all_to_all x1, waiting for transfers between devices, on_device(): lax.all_to_all(produced, 'tok', split_axis=0, concat_axis=0, tiled=True)  276 us
    all_gather x1, waiting for transfers between devices, on_device(): lax.all_gather(output_proj, 'tok', axis=1, tiled=True)  139 us
    reduce_scatter x1, waiting for transfers between devices, on_device(): lax.psum_scatter(partial_sums, 'kv', scatter_dimension=0, tiled=True)  36.4 us
  transfers between devices with their start and end apart: 3, of which 3 were waited for; matrix products, arithmetic and copies ran while one was open for 1% of the time, Pallas kernels for 0%

commit v1 on v0

v1 whole, which is shorter than its diff:
```python
import jax
import jax.numpy as jnp
from jax import lax
from jax.sharding import PartitionSpec as P

HD = 128
EXPERTS = 64
TOPK = 6
CAP = 16


def visible_mask(length, first_visible, span_rows, cached):
    cache_pos = jnp.arange(cached, dtype=jnp.int32)
    cache_ok = jnp.logical_and(cache_pos >= first_visible, cache_pos < length)
    position = jnp.arange(span_rows, dtype=jnp.int32)
    causal = position[None, :] <= position[:, None]
    return jnp.concatenate(
        [jnp.broadcast_to(cache_ok[None, :], (span_rows, cached)), causal], axis=1
    )


def attend_heads(query_rows, all_keys, all_values, allowed):
    head_count = query_rows.shape[1] // HD
    score_scale = HD ** (-0.5)
    results = []
    for head_index in range(head_count):
        query_block = query_rows[:, head_index * HD : (head_index + 1) * HD]
        scores = jnp.dot(query_block, all_keys.T, preferred_element_type=jnp.float32) * score_scale
        scores = jnp.where(allowed, scores, -1e30)
        largest = jnp.max(scores, axis=1, keepdims=True)
        exponent = jnp.exp(scores - largest)
        attention_weights = (exponent / jnp.sum(exponent, axis=1, keepdims=True)).astype(
            jnp.bfloat16
        )
        results.append(
            jnp.dot(attention_weights, all_values, preferred_element_type=jnp.float32).astype(
                jnp.bfloat16
            )
        )
    return jnp.concatenate(results, axis=1)


def tok_groups(members):
    chips_z = members // 8
    along_z = [
        [(y * chips_z + z) * 2 + core for z in range(chips_z)]
        for y in range(4)
        for core in range(2)
    ]
    across = [
        [(y * chips_z + z) * 2 + core for y in range(4) for core in range(2)]
        for z in range(chips_z)
    ]
    return along_z, across


def slot_tables(table, first_expert):
    blocks, _, rows = table.shape
    experts = jnp.stack(
        [first_expert, first_expert + 1, first_expert + 32, first_expert + 33]
    ).astype(jnp.float32)
    named = table[:, None, :TOPK, :] == experts[None, :, None, None]
    member = jnp.any(named, axis=2)
    weight = jnp.sum(jnp.where(named, table[:, None, TOPK:, :], 0.0), axis=2)
    earlier = (
        jnp.arange(rows, dtype=jnp.int32)[:, None] < jnp.arange(rows, dtype=jnp.int32)[None, :]
    ).astype(jnp.bfloat16)
    rank = jnp.dot(
        member.astype(jnp.bfloat16).reshape(blocks * 4, rows),
        earlier,
        preferred_element_type=jnp.float32,
    ).reshape(blocks, 4, rows)
    slots = jnp.arange(CAP, dtype=jnp.int32).astype(jnp.float32)
    chosen = jnp.logical_and(
        member[:, :, None, :], rank[:, :, None, :] == slots[None, None, :, None]
    )
    slot_weight = jnp.sum(jnp.where(chosen, weight[:, :, None, :], 0.0), axis=3)
    return chosen.astype(jnp.bfloat16), slot_weight


def run_experts(normed_rows, chosen, slot_weight, gate_up, down):
    blocks, rows, width = normed_rows.shape
    grouped = jnp.einsum(
        "bect,btd->ebcd", chosen, normed_rows, preferred_element_type=jnp.float32
    ).astype(jnp.bfloat16)
    grouped = grouped.reshape(4, blocks * CAP, width)
    half = down.shape[1]
    produced = []
    for expert in range(4):
        total = None
        for part in range(2):
            piece = part * 4 + expert
            both = jnp.dot(grouped[expert], gate_up[piece], preferred_element_type=jnp.float32)
            hidden = (jax.nn.silu(both[:, :half]) * both[:, half:]).astype(jnp.bfloat16)
            out = jnp.dot(hidden, down[piece], preferred_element_type=jnp.float32)
            total = out if total is None else total + out
        scale = slot_weight[:, expert, :].reshape(blocks * CAP, 1)
        produced.append((total * scale).astype(jnp.bfloat16).reshape(blocks, CAP, width))
    stacked = jnp.stack(produced, axis=1)
    return jnp.einsum(
        "bect,becd->btd", chosen, stacked, preferred_element_type=jnp.float32
    ).astype(jnp.bfloat16)


def on_device(
    layer_input,
    queries,
    keys_new,
    values_new,
    cache_keys,
    cache_values,
    cache_length,
    cache_start,
    output_proj,
    norm_gain,
    expert_routes,
    route_weights,
    piece_gate_up,
    piece_down,
):
    span_rows = queries.shape[1]
    cached = cache_keys.shape[1]
    allowed = visible_mask(cache_length[0], cache_start[0], span_rows, cached)
    all_keys = jnp.concatenate([cache_keys[0], keys_new[0]], axis=0)
    all_values = jnp.concatenate([cache_values[0], values_new[0]], axis=0)
    attended = attend_heads(queries[0], all_keys, all_values, allowed)
    members = lax.axis_size("tok")
    along_z, across = tok_groups(members)
    chips_z = members // 8
    rows_out, cols_own = output_proj.shape
    model_width = layer_input.shape[2]
    table = jnp.concatenate(
        [expert_routes[0].astype(jnp.float32).T, route_weights[0].T], axis=0
    )
    table = lax.all_gather(table, "tok", axis=0, axis_index_groups=along_z)
    proj = lax.all_gather(output_proj.T, "tok", axis=0, axis_index_groups=along_z)
    proj = lax.all_gather(proj, "tok", axis=0, axis_index_groups=across)
    proj = (
        proj.reshape(4, 2, chips_z, cols_own, rows_out)
        .transpose(0, 2, 1, 3, 4)
        .reshape(model_width, rows_out)
    )
    gate_up = lax.all_gather(piece_gate_up[0], "tok", axis=0, axis_index_groups=across)
    down = lax.all_gather(piece_down[0], "tok", axis=0, axis_index_groups=across)
    partial_sums = lax.dot_general(
        attended, proj, (((1,), (1,)), ((), ())), preferred_element_type=jnp.float32
    )
    attention = lax.psum_scatter(partial_sums, "kv", scatter_dimension=0, tiled=True)
    residual = layer_input[0].astype(jnp.float32) + attention
    normed = (
        residual
        * lax.rsqrt(jnp.mean(residual * residual, axis=1, keepdims=True) + 1e-05)
        * norm_gain
    ).astype(jnp.bfloat16)
    first_expert = 2 * (lax.axis_index("tok") // 2 % chips_z)
    chosen, slot_weight = slot_tables(table, first_expert)
    normed_rows = lax.all_gather(normed, "tok", axis=0, axis_index_groups=along_z)
    sums = run_experts(normed_rows, chosen, slot_weight, gate_up, down)
    routed_sum = lax.psum_scatter(
        sums, "tok", scatter_dimension=0, axis_index_groups=along_z, tiled=False
    )
    return (residual + routed_sum.astype(jnp.float32)).astype(jnp.bfloat16)[None]


def solution(mesh):
    return jax.shard_map(
        on_device,
        mesh=mesh,
        in_specs=(
            P("tok", "kv", None),
            P("tok", None, "kv"),
            P("tok", None, "kv"),
            P("tok", None, "kv"),
            P("tok", None, "kv"),
            P("tok", None, "kv"),
            P("tok"),
            P("tok"),
            P("kv", "tok"),
            P(),
            P("tok", "kv", None),
            P("tok", "kv", None),
            P("tok", None, None),
            P("tok", None, None),
        ),
        out_specs=P("tok", "kv", None),
        check_vma=False,
    )
```

time: 849 us -> 447 us (0.53)
  blocking collectives: 295 us -> 68.9 us
  waiting for transfers between devices: 453 us -> 310 us
  local copies, waits for them, and re-layouts: 35.5 us -> 4.94 us
  matrix products: 20.6 us -> 39.1 us
  starting transfers between devices: 9.68 us -> 0.2 us
  other arithmetic: 16.5 us -> 7.4 us
    all_to_all x1 -> x0, blocking collectives: 295 us -> none  [on_device(): lax.all_to_all(outgoing, 'tok', split_axis=0, concat_axis=0, tiled=True)]
    all_to_all x1 -> x0, waiting for transfers between devices: 276 us -> none  [on_device(): lax.all_to_all(produced, 'tok', split_axis=0, concat_axis=0, tiled=True)]
    reduce_scatter x0 -> x1, waiting for transfers between devices: none -> 88.9 us  [on_device(): lax.psum_scatter(sums, 'tok', scatter_dimension=0, axis_index_groups=alon...]
    all_gather x0 -> x2, blocking collectives: none -> 68.9 us  [the longest x1 36.8 us: on_device(): lax.all_gather(output_proj.T, 'tok', axis=0, axis_index_groups=along_z)]
    all_gather x1 -> x4, waiting for transfers between devices: 139 us -> 176 us  [the longest x1 69.6 us: on_device(): lax.all_gather(piece_gate_up[0], 'tok', axis=0, axis_index_groups=across)]
    gather x2 -> x0, local copies, waits for them, and re-layouts: 19.1 us -> none  [the longest x1 9.57 us: on_device(): second_half = jnp.take(flat_back, places + EXPERTS * CAP, axis=0)]
    dot_general x4 -> x20, matrix products: 14.5 us -> 33.1 us  [the longest x8 15.1 us: run_experts(): jnp.dot(grouped[expert], gate_up[piece], preferred_element_type=jnp.float32)]
    all_to_all x1 -> x0, starting transfers between devices: 9.61 us -> none  [on_device(): lax.all_to_all(produced, 'tok', split_axis=0, concat_axis=0, tiled=True)]
  transfers between devices with their start and end apart: 3 -> 6, of which waited for: 3 -> 6; matrix products, arithmetic and copies ran while one was open for 1% -> 7% of each run, Pallas kernels for 0% -> 0%
where the time goes in v1:
time: 447 us; the launch traced here: 446 us
  waiting for transfers between devices  310 us (69%)
  blocking collectives  68.9 us (15%)
  matrix products  39.1 us (9%)
  between operations  15.2 us (3%)
  other arithmetic  7.4 us (2%)
  local copies, waits for them, and re-layouts  4.94 us (1%)
    reduce_scatter x1, waiting for transfers between devices, on_device(): lax.psum_scatter(sums, 'tok', scatter_dimension=0, axis_index_groups=alon...  88.9 us
    all_gather x1, waiting for transfers between devices, on_device(): lax.all_gather(piece_gate_up[0], 'tok', axis=0, axis_index_groups=across)  69.6 us
    all_gather x1, waiting for transfers between devices, on_device(): lax.all_gather(normed, 'tok', axis=0, axis_index_groups=along_z)  52.4 us
    reduce_scatter x1, waiting for transfers between devices, on_device(): lax.psum_scatter(partial_sums, 'kv', scatter_dimension=0, tiled=True)  44.3 us
    all_gather x1, blocking collectives, on_device(): lax.all_gather(output_proj.T, 'tok', axis=0, axis_index_groups=along_z)  36.8 us
    all_gather x1, waiting for transfers between devices, on_device(): lax.all_gather(piece_down[0], 'tok', axis=0, axis_index_groups=across)  35.9 us
    all_gather x1, blocking collectives, on_device(): table = lax.all_gather(table, 'tok', axis=0, axis_index_groups=along_z)  32.1 us
    all_gather x1, waiting for transfers between devices, on_device(): proj = lax.all_gather(proj, 'tok', axis=0, axis_index_groups=across)  18.2 us
  transfers between devices with their start and end apart: 6, of which 6 were waited for; matrix products, arithmetic and copies ran while one was open for 7% of the time, Pallas kernels for 0%

profile of v1, /device:TPU:6, one launch (start us, length us, event | category | flops | bytes accessed | tf_op | source)
XLA Modules:
  0.0 446.3 jit_solution(9970218011489379940)
XLA Ops:
  6.5 36.8 %all-gather.4 = bf16[16,12,384]{2,1,0:T(8,128)(2,1)S(1)} all-gather(bf16[1,12,384]{2,1,0:T(8,128)(2,1)} %bitcast.160), channel_id=2, replica_groups={{0,2,4,6,8,10,12,14,16,18,20,22,24,26,28,30},{1,3,5,7,9,11,13,15,17,19,..., dimensions={0}, use_global_device_ids=true | all-gather | bytes 156672 | tf_op jit(solution)/shard_map/all_gather | solution.py:136
  45.5 2.6 fusion.110
  53.2 18.2 %all-gather.15.cloned.1.call-done = bf16[128,12,384]{2,0,1:T(8,128)(2,1)} async-done(((bf16[16,12,384]{2,0,1:T(8,128)(2,1)}), bf16[128,12,384]{2,0,1:T(8,128)(2,1)}) %all-gather.15.cloned.1.call-update) | async-done | bytes 1179664 | tf_op jit(solution)/shard_map/all_gather | solution.py:137
  71.3 2.0 copy.59
  73.7 2.7 fusion.45
  76.5 44.3 %reduce-scatter.3.cloned.1.call-done = f32[128,1536]{1,0:T(8,128)} async-done(((f32[512,1536]{1,0:T(8,128)}), f32[128,1536]{1,0:T(8,128)}) %reduce-scatter.3.cloned.1.call-update) | async-done | bytes 786448 | tf_op jit(solution)/shard_map/reduce_scatter | solution.py:148
  122.1 2.0 multiply_convert_fusion
  125.4 32.1 %all-gather.5 = f32[16,12,128]{2,1,0:T(8,128)S(1)} all-gather(f32[1,12,128]{2,1,0:T(8,128)S(1)} %maximum_bitcast_fusion), channel_id=4, replica_groups={{0,2,4,6,8,10,12,14,16,18,20,22,24,26,28,30},{1,3,5,7,9,11,13,15,17,19,..., dimensions={0}, use_global_device_ids=true | all-gather | bytes 104448 | tf_op jit(solution)/shard_map/all_gather | solution.py:135
  160.0 52.4 %all-gather.17.cloned.1.call-done = bf16[2048,1536]{1,0:T(8,128)(2,1)} async-done(((bf16[128,1536]{1,0:T(8,128)(2,1)}), bf16[2048,1536]{1,0:T(8,128)(2,1)}) %all-gather.17.cloned.1.call-update) | async-done | bytes 6291472 | tf_op jit(solution)/shard_map/all_gather | solution.py:157
  212.4 3.8 fusion.6
  216.5 69.6 %all-gather.11.cloned.1.call-done = bf16[8,1536,512]{2,1,0:T(8,128)(2,1)} async-done(((bf16[1,1536,512]{2,1,0:T(8,128)(2,1)}), bf16[8,1536,512]{2,1,0:T(8,128)(2,1)}) %all-gather.11.cloned.1.call-update) | async-done | bytes 12582928 | tf_op jit(solution)/shard_map/all_gather | solution.py:143
  286.1 2.9 fusion.32
  289.0 3.5 fusion.31
  292.5 2.8 fusion.30
  295.3 2.0 fusion.29
  297.3 1.4 fusion.28
  299.2 1.4 fusion.26
  301.2 35.9 %all-gather.13.cloned.1.call-done = bf16[8,256,1536]{2,1,0:T(8,128)(2,1)} async-done(((bf16[1,256,1536]{2,1,0:T(8,128)(2,1)}), bf16[8,256,1536]{2,1,0:T(8,128)(2,1)}) %all-gather.13.cloned.1.call-update) | async-done | bytes 6291472 | tf_op jit(solution)/shard_map/all_gather | solution.py:144
  337.0 1.8 fusion.42
  338.9 2.1 fusion.41
  341.0 1.6 fusion.40
  344.7 3.9 bitcast_convert_fusion
  348.6 88.9 %reduce-scatter.5.cloned.1.call-done = bf16[1,128,1536]{2,1,0:T(8,128)(2,1)} async-done(((bf16[16,128,1536]{2,1,0:T(8,128)(2,1)}), bf16[1,128,1536]{2,1,0:T(8,128)(2,1)}) %reduce-scatter.5.cloned.1.call-update) | async-done | bytes 393232 | tf_op jit(solution)/shard_map/reduce_scatter | solution.py:159
  437.5 1.9 fusion.44
  (97 shorter events, 14.5 us)
Async XLA Ops:
  6.5 41.6 %copy-start.17 = (bf16[1,1024,128]{2,1,0:T(8,128)(2,1)S(1)}, bf16[1,1024,128]{2,1,0:T(8,128)(2,1)}, u32[]{:S(2)}) copy-start(bf16[1,1024,128]{2,1,0:T(8,128)(2,1)} %param.18) | copy-start | bytes 786436
  6.5 41.6 %copy-start.19 = (bf16[1,512,128]{2,1,0:T(8,128)(2,1)S(1)}, bf16[1,512,128]{2,1,0:T(8,128)(2,1)}, u32[]{:S(2)}) copy-start(bf16[1,512,128]{2,1,0:T(8,128)(2,1)} %param.16) | copy-start | bytes 393220
  6.5 41.6 %copy-start.16 = (bf16[1,512,384]{2,1,0:T(8,128)(2,1)S(1)}, bf16[1,512,384]{2,1,0:T(8,128)(2,1)}, u32[]{:S(2)}) copy-start(bf16[1,512,384]{2,1,0:T(8,128)(2,1)} %param.15) | copy-start | bytes 1179652
  6.5 64.8 %all-gather.15.cloned.1.call-start = ((), (), s32[]{:S(2)}) async-start(), calls=%async_computation.6 | async-start | bytes 1327104 | tf_op jit(solution)/shard_map/all_gather | solution.py:137
  44.1 76.7 %reduce-scatter.3.cloned.1.call-start = ((), (), s32[]{:S(2)}) async-start(), calls=%async_computation.2 | async-start | bytes 3932160 | tf_op jit(solution)/shard_map/reduce_scatter | solution.py:148
  50.0 1.0 copy-start.18
  50.0 1.0 copy-start.20
  76.4 44.4 %copy-start.2 = (bf16[1,128,1536]{2,1,0:T(8,128)(2,1)S(1)}, bf16[1,128,1536]{2,1,0:T(8,128)(2,1)}, u32[]{:S(2)}) copy-start(bf16[1,128,1536]{2,1,0:T(8,128)(2,1)} %param.14) | copy-start | bytes 1179652
  76.4 45.7 %copy-start.8 = (f32[1536]{0:T(1024)S(1)}, f32[1536]{0:T(1024)}, u32[]{:S(2)}) copy-start(f32[1536]{0:T(1024)} %param.23) | copy-start | bytes 18436
  76.4 49.0 %copy-start.11 = (f32[1,128,6]{1,0,2:T(1,128)S(1)}, f32[1,128,6]{1,0,2:T(1,128)}, u32[]{:S(2)}) copy-start(f32[1,128,6]{1,0,2:T(1,128)} %param.25) | copy-start | bytes 9220
  76.4 49.0 %copy-start.12 = (s32[1,128,6]{1,0,2:T(1,128)S(1)}, s32[1,128,6]{1,0,2:T(1,128)}, u32[]{:S(2)}) copy-start(s32[1,128,6]{1,0,2:T(1,128)} %param.24) | copy-start | bytes 9220
  76.4 136.0 %all-gather.17.cloned.1.call-start = ((), (), s32[]{:S(2)}) async-start(), calls=%async_computation.7 | async-start | bytes 6684672 | tf_op jit(solution)/shard_map/all_gather | solution.py:157
  124.1 161.9 %all-gather.11.cloned.1.call-start = ((), (), s32[]{:S(2)}) async-start(), calls=%async_computation.3 | async-start | bytes 14155776 | tf_op jit(solution)/shard_map/all_gather | solution.py:143
  124.7 212.3 %all-gather.13.cloned.1.call-start = ((), (), s32[]{:S(2)}) async-start(), calls=%async_computation.4 | async-start | bytes 7077888 | tf_op jit(solution)/shard_map/all_gather | solution.py:144
  125.3 312.2 %reduce-scatter.5.cloned.1.call-start = ((), (), s32[]{:S(2)}) async-start(), calls=%async_computation.5 | async-start | bytes 6684672 | tf_op jit(solution)/shard_map/reduce_scatter | solution.py:159
  157.9 54.5 %copy-start.6 = (f32[16,4,128]{2,1,0:T(4,128)}, f32[16,4,128]{2,1,0:T(4,128)S(1)}, u32[]{:S(2)}) copy-start(f32[16,4,128]{2,1,0:T(4,128)S(1)} %copy.44) | copy-start | bytes 98308
  158.1 54.3 %copy-start.13 = (f32[16]{0:T(128)}, f32[16]{0:T(128)S(1)}, u32[]{:S(2)}) copy-start(f32[16]{0:T(128)S(1)} %iota_convert_fusion) | copy-start | bytes 196
  286.1 11.2 %copy-start.15 = (bf16[8,1536,512]{2,1,0:T(8,128)(2,1)S(1)}, bf16[8,1536,512]{2,1,0:T(8,128)(2,1)}, u32[]{:S(2)}) copy-start(bf16[8,1536,512]{2,1,0:T(8,128)(2,1)} %all-gather.11.cloned.1.call-done) | copy-start | bytes 37748740
  301.2 39.8 %copy-start.4 = (f32[256,512]{1,0:T(8,128)S(1)}, f32[256,512]{1,0:T(8,128)}, u32[]{:S(2)}) copy-start(f32[256,512]{1,0:T(8,128)} %fusion.28) | copy-start | bytes 1572868
  337.0 5.5 %copy-start.1 = (bf16[8,256,1536]{2,1,0:T(8,128)(2,1)S(1)}, bf16[8,256,1536]{2,1,0:T(8,128)(2,1)}, u32[]{:S(2)}) copy-start(bf16[8,256,1536]{2,1,0:T(8,128)(2,1)} %all-gather.13.cloned.1.call-done) | copy-start | bytes 18874372
  338.9 3.7 copy-start.5
  341.0 2.0 copy-start.3
  341.0 2.0 copy-start.10
  348.6 89.0 %copy-start = (f32[128,1536]{1,0:T(8,128)S(1)}, f32[128,1536]{1,0:T(8,128)}, u32[]{:S(2)}) copy-start(f32[128,1536]{1,0:T(8,128)} %reduce-scatter.3.cloned.1.call-done) | copy-start | bytes 2359300
  (3 other events, 2.5 us)
Sparse Core Ops, SparseCore 0:
  44.2 27.1 all-gather.14
  76.5 44.2 reduce-scatter.2
  124.3 88.0 all-gather.16
  214.4 71.6 all-gather.10
  288.0 48.9 all-gather.12
  348.7 88.7 reduce-scatter.4

commit v2 on v1

--- a/solution.py
+++ b/solution.py
@@ -1,6 +1,10 @@
+import functools
+
 import jax
 import jax.numpy as jnp
 from jax import lax
+from jax.experimental import pallas as pl
+from jax.experimental.pallas import tpu as pltpu
 from jax.sharding import PartitionSpec as P
 
 HD = 128
@@ -42,16 +46,10 @@
 
 def tok_groups(members):
     chips_z = members // 8
-    along_z = [
-        [(y * chips_z + z) * 2 + core for z in range(chips_z)]
-        for y in range(4)
-        for core in range(2)
-    ]
-    across = [
+    return [
         [(y * chips_z + z) * 2 + core for y in range(4) for core in range(2)]
         for z in range(chips_z)
     ]
-    return along_z, across
 
 
 def slot_tables(table, first_expert):
@@ -100,6 +98,240 @@
     return jnp.einsum(
         "bect,becd->btd", chosen, stacked, preferred_element_type=jnp.float32
     ).astype(jnp.bfloat16)
+
+
+MESH = pl.DeviceIdType.MESH
+
+
+def spot(chips_z):
+    here = lax.axis_index("tok")
+    y, z, core = here // (2 * chips_z), (here // 2) % chips_z, here % 2
+
+    def index(y, z, core):
+        return (y * chips_z + z) * 2 + core
+
+    return y, z, core, index
+
+
+def greet(peers):
+    barrier = pltpu.get_barrier_semaphore()
+    for peer in peers:
+        pl.semaphore_signal(barrier, inc=1, device_id=peer, device_id_type=MESH)
+    pl.semaphore_wait(barrier, len(peers))
+
+
+def params_kernel(chips_z, shard_ref, table_ref, proj_ref, tables_ref,
+                  zs, zr, ts, tr, ys, yr, cs, cr):
+    y, z, core, index = spot(chips_z)
+    far = [(z + d) % chips_z for d in range(1, chips_z)]
+    beside = [(y + d) % 4 for d in range(1, 4)]
+    partner = {"tok": index(y, z, 1 - core)}
+    peers = [{"tok": index(y, other, core)} for other in far]
+    peers += [{"tok": index(other, z, core)} for other in beside] + [partner]
+    greet(peers)
+
+    def push(src, dst, send, recv, target):
+        return pltpu.make_async_remote_copy(
+            src_ref=src, dst_ref=dst, send_sem=send, recv_sem=recv,
+            device_id=target, device_id_type=MESH,
+        )
+
+    shards = []
+    order = sorted(range(chips_z - 1), key=lambda d: -min(d + 1, chips_z - 1 - d))
+    for d in order:
+        shards.append(
+            push(shard_ref, proj_ref.at[core, y, z], zs.at[d], zr.at[d], peers[d])
+        )
+        shards[-1].start()
+    for d in order:
+        shards.append(push(table_ref, tables_ref.at[z], ts.at[d], tr.at[d], peers[d]))
+        shards[-1].start()
+    proj_ref[core, y, z] = shard_ref[...]
+    tables_ref[z] = table_ref[...]
+    for copy in shards[: chips_z - 1]:
+        copy.wait_recv()
+    columns = []
+    for d, other in enumerate(beside):
+        block = proj_ref.at[core, y]
+        columns.append(
+            push(block, block, ys.at[d], yr.at[d], {"tok": index(other, z, core)})
+        )
+        columns[-1].start()
+    halves = []
+    for d in range(4):
+        if d > 0:
+            columns[d - 1].wait_recv()
+        block = proj_ref.at[core, (y + 4 - d) % 4]
+        halves.append(push(block, block, cs.at[d], cr.at[d], partner))
+        halves[-1].start()
+    for copy in shards[chips_z - 1 :]:
+        copy.wait_recv()
+    for copy in halves:
+        copy.wait_recv()
+    for copy in shards + columns + halves:
+        copy.wait_send()
+
+
+def gather_params(shard, table, chips_z):
+    cols, rows = shard.shape
+    dma = pltpu.SemaphoreType.DMA
+    vmem = pl.BlockSpec(memory_space=pltpu.VMEM)
+    return pl.pallas_call(
+        functools.partial(params_kernel, chips_z),
+        out_shape=(
+            jax.ShapeDtypeStruct((2, 4, chips_z, cols, rows), shard.dtype),
+            jax.ShapeDtypeStruct((chips_z,) + table.shape, table.dtype),
+        ),
+        in_specs=[vmem, vmem],
+        out_specs=(vmem, vmem),
+        scratch_shapes=[dma((chips_z - 1,))] * 4 + [dma((3,))] * 2 + [dma((4,))] * 2,
+        compiler_params=pltpu.CompilerParams(collective_id=0, has_side_effects=True),
+    )(shard, table)
+
+
+def ring_chunks(chips_z, step):
+    if step < chips_z // 2 - 1:
+        return [(0, 0), (1, 1), (0, 1), (1, 0)]
+    return [(0, 0), (1, 1)]
+
+
+def norm_kernel(chips_z, kv_count, parts_ref, input_ref, gain_ref, residual_ref, rows_ref,
+                got, xs, xr, zs, zr):
+    y, z, core, index = spot(chips_z)
+    me = lax.axis_index("kv")
+    half = input_ref.shape[0] // 2
+    owners = [(me + d) % kv_count for d in range(1, kv_count)]
+    steps = ((z + 1) % chips_z, (z + chips_z - 1) % chips_z)
+    sides = [{"tok": index(y, other, core)} for other in steps]
+    greet([{"kv": other} for other in owners] + sides)
+    shares = {}
+    for chunk in range(2):
+        span = pl.ds(chunk * half, half)
+        for d in sorted(range(kv_count - 1), key=lambda d: -min(d + 1, kv_count - 1 - d)):
+            shares[d, chunk] = pltpu.make_async_remote_copy(
+                src_ref=parts_ref.at[owners[d], span], dst_ref=got.at[d, span],
+                send_sem=xs.at[d, chunk], recv_sem=xr.at[d, chunk],
+                device_id={"kv": owners[d]}, device_id_type=MESH,
+            )
+            shares[d, chunk].start()
+
+    moves = {}
+
+    def move(direction, step, chunk):
+        block = (z + chips_z - step) % chips_z if direction == 0 else (z + step) % chips_z
+        ref = rows_ref.at[block, pl.ds(chunk * half, half)]
+        moves[direction, step, chunk] = pltpu.make_async_remote_copy(
+            src_ref=ref, dst_ref=ref,
+            send_sem=zs.at[direction, step, chunk], recv_sem=zr.at[direction, step, chunk],
+            device_id=sides[direction], device_id_type=MESH,
+        )
+        moves[direction, step, chunk].start()
+
+    for chunk in range(2):
+        for d in range(kv_count - 1):
+            shares[d, chunk].wait_recv()
+
+        def tile(i, carry):
+            span = pl.ds(pl.multiple_of(chunk * half + i * 16, 16), 16)
+            total = parts_ref[me, span].astype(jnp.float32)
+            for d in range(kv_count - 1):
+                total = total + got[d, span].astype(jnp.float32)
+            total = total + input_ref[span].astype(jnp.float32)
+            residual_ref[span] = total
+            mean = jnp.mean(total * total, axis=1, keepdims=True)
+            rows_ref[z, span] = (total * lax.rsqrt(mean + 1e-05) * gain_ref[...]).astype(
+                jnp.bfloat16
+            )
+            return carry
+
+        lax.fori_loop(0, half // 16, tile, 0)
+        for direction, part in ring_chunks(chips_z, 0):
+            if part == chunk:
+                move(direction, 0, chunk)
+    for step in range(1, chips_z // 2):
+        for direction, chunk in ring_chunks(chips_z, step):
+            moves[direction, step - 1, chunk].wait_recv()
+            move(direction, step, chunk)
+    last = chips_z // 2 - 1
+    for direction, chunk in ((0, 1), (1, 0)):
+        moves[direction, last - 1, chunk].wait_recv()
+    for direction, chunk in ring_chunks(chips_z, last):
+        moves[direction, last, chunk].wait_recv()
+    for copy in list(shares.values()) + list(moves.values()):
+        copy.wait_send()
+
+
+def norm_and_gather(parts, layer_rows, gain, chips_z):
+    kv_count, rows, width = parts.shape
+    dma = pltpu.SemaphoreType.DMA
+    vmem = pl.BlockSpec(memory_space=pltpu.VMEM)
+    return pl.pallas_call(
+        functools.partial(norm_kernel, chips_z, kv_count),
+        out_shape=(
+            jax.ShapeDtypeStruct((rows, width), jnp.float32),
+            jax.ShapeDtypeStruct((chips_z, rows, width), jnp.bfloat16),
+        ),
+        in_specs=[vmem] * 3,
+        out_specs=(vmem, vmem),
+        scratch_shapes=[pltpu.VMEM((kv_count - 1, rows, width), jnp.bfloat16)]
+        + [dma((kv_count - 1, 2))] * 2
+        + [dma((2, chips_z // 2, 2))] * 2,
+        compiler_params=pltpu.CompilerParams(collective_id=1, has_side_effects=True),
+    )(parts, layer_rows, gain)
+
+
+def return_kernel(chips_z, sums_ref, residual_ref, out_ref, arrived, ss, sr):
+    y, z, core, index = spot(chips_z)
+    half = residual_ref.shape[0] // 2
+    reach = chips_z // 2
+    steps = ((z + 1) % chips_z, (z + chips_z - 1) % chips_z)
+    sides = [{"tok": index(y, other, core)} for other in steps]
+    greet(sides)
+    moves = {}
+    for step in range(reach):
+        for direction, chunk in ring_chunks(chips_z, reach - 1 - step):
+            ahead = reach - step
+            target = (z + ahead) % chips_z if direction == 0 else (z + chips_z - ahead) % chips_z
+            span = pl.ds(chunk * half, half)
+            source = sums_ref.at[target, span]
+            if (direction, step - 1, chunk) in moves:
+                moves[direction, step - 1, chunk].wait_recv()
+                held = arrived.at[direction, step - 1]
+                held[span] = (
+                    held[span].astype(jnp.float32)
+                    + sums_ref[target, span].astype(jnp.float32)
+                ).astype(jnp.bfloat16)
+                source = arrived.at[direction, step - 1, span]
+            moves[direction, step, chunk] = pltpu.make_async_remote_copy(
+                src_ref=source, dst_ref=arrived.at[direction, step, span],
+                send_sem=ss.at[direction, step, chunk], recv_sem=sr.at[direction, step, chunk],
+                device_id=sides[direction], device_id_type=MESH,
+            )
+            moves[direction, step, chunk].start()
+    for chunk in range(2):
+        span = pl.ds(chunk * half, half)
+        total = residual_ref[span] + sums_ref[z, span].astype(jnp.float32)
+        for direction in range(2):
+            moves[direction, reach - 1, chunk].wait_recv()
+            total = total + arrived[direction, reach - 1, span].astype(jnp.float32)
+        out_ref[span] = total.astype(jnp.bfloat16)
+    for copy in moves.values():
+        copy.wait_send()
+
+
+def return_sums(sums, residual, chips_z):
+    rows, width = residual.shape
+    dma = pltpu.SemaphoreType.DMA
+    vmem = pl.BlockSpec(memory_space=pltpu.VMEM)
+    return pl.pallas_call(
+        functools.partial(return_kernel, chips_z),
+        out_shape=jax.ShapeDtypeStruct((rows, width), jnp.bfloat16),
+        in_specs=[vmem, vmem],
+        out_specs=vmem,
+        scratch_shapes=[pltpu.VMEM((2, chips_z // 2, rows, width), jnp.bfloat16)]
+        + [dma((2, chips_z // 2, 2))] * 2,
+        compiler_params=pltpu.CompilerParams(collective_id=2, has_side_effects=True),
+    )(sums, residual)
 
 
 def on_device(
@@ -125,41 +357,35 @@
     all_values = jnp.concatenate([cache_values[0], values_new[0]], axis=0)
     attended = attend_heads(queries[0], all_keys, all_values, allowed)
     members = lax.axis_size("tok")
-    along_z, across = tok_groups(members)
+    kv_count = lax.axis_size("kv")
+    across = tok_groups(members)
     chips_z = members // 8
     rows_out, cols_own = output_proj.shape
     model_width = layer_input.shape[2]
+    gate_up = lax.all_gather(piece_gate_up[0], "tok", axis=0, axis_index_groups=across)
+    down = lax.all_gather(piece_down[0], "tok", axis=0, axis_index_groups=across)
     table = jnp.concatenate(
         [expert_routes[0].astype(jnp.float32).T, route_weights[0].T], axis=0
     )
-    table = lax.all_gather(table, "tok", axis=0, axis_index_groups=along_z)
-    proj = lax.all_gather(output_proj.T, "tok", axis=0, axis_index_groups=along_z)
-    proj = lax.all_gather(proj, "tok", axis=0, axis_index_groups=across)
+    proj, table = gather_params(output_proj.T, table, chips_z)
     proj = (
-        proj.reshape(4, 2, chips_z, cols_own, rows_out)
-        .transpose(0, 2, 1, 3, 4)
+        proj.reshape(2, 4, chips_z, cols_own, rows_out)
+        .transpose(1, 2, 0, 3, 4)
         .reshape(model_width, rows_out)
     )
-    gate_up = lax.all_gather(piece_gate_up[0], "tok", axis=0, axis_index_groups=across)
-    down = lax.all_gather(piece_down[0], "tok", axis=0, axis_index_groups=across)
     partial_sums = lax.dot_general(
         attended, proj, (((1,), (1,)), ((), ())), preferred_element_type=jnp.float32
-    )
-    attention = lax.psum_scatter(partial_sums, "kv", scatter_dimension=0, tiled=True)
-    residual = layer_input[0].astype(jnp.float32) + attention
-    normed = (
-        residual
-        * lax.rsqrt(jnp.mean(residual * residual, axis=1, keepdims=True) + 1e-05)
-        * norm_gain
     ).astype(jnp.bfloat16)
+    residual, normed_rows = norm_and_gather(
+        partial_sums.reshape(kv_count, span_rows // kv_count, model_width),
+        layer_input[0],
+        norm_gain[None],
+        chips_z,
+    )
     first_expert = 2 * (lax.axis_index("tok") // 2 % chips_z)
     chosen, slot_weight = slot_tables(table, first_expert)
-    normed_rows = lax.all_gather(normed, "tok", axis=0, axis_index_groups=along_z)
     sums = run_experts(normed_rows, chosen, slot_weight, gate_up, down)
-    routed_sum = lax.psum_scatter(
-        sums, "tok", scatter_dimension=0, axis_index_groups=along_z, tiled=False
-    )
-    return (residual + routed_sum.astype(jnp.float32)).astype(jnp.bfloat16)[None]
+    return return_sums(sums, residual, chips_z)[None]
 
 
 def solution(mesh):

time: 447 us -> 277 us (0.62)
  waiting for transfers between devices: 310 us -> 1.45 us
  Pallas kernels: 0 us -> 212 us
  blocking collectives: 68.9 us -> 0 us
    pallas_call x0 -> x3, Pallas kernels: none -> 212 us  [the longest x1 89.4 us: norm_and_gather(): pl.pallas_call(functools.partial(norm_kernel, chips_z, kv_count), out_sha...]
    reduce_scatter x2 -> x0, waiting for transfers between devices: 133 us -> none  [the longest x1 88.9 us: on_device(): lax.psum_scatter(sums, 'tok', scatter_dimension=0, axis_index_groups=alon...]
    all_gather x2 -> x0, waiting for transfers between devices: 70.6 us -> none  [the longest x1 52.4 us: on_device(): lax.all_gather(normed, 'tok', axis=0, axis_index_groups=along_z)]
    all_gather x1, waiting for transfers between devices: 69.6 us -> 0.02 us  [on_device(): lax.all_gather(piece_gate_up[0], 'tok', axis=0, axis_index_groups=across)]
    all_gather x2 -> x0, blocking collectives: 68.9 us -> none  [the longest x1 36.8 us: on_device(): lax.all_gather(output_proj.T, 'tok', axis=0, axis_index_groups=along_z)]
    all_gather x1, waiting for transfers between devices: 35.9 us -> 0.02 us  [on_device(): lax.all_gather(piece_down[0], 'tok', axis=0, axis_index_groups=across)]
  transfers between devices with their start and end apart: 6 -> 2, of which waited for: 6 -> 0; matrix products, arithmetic and copies ran while one was open for 7% -> 13% of each run, Pallas kernels for 0% -> 51%
where the time goes in v2:
time: 277 us
  Pallas kernels  212 us (77%)
  matrix products  37.7 us (14%)
  between operations  15.1 us (5%)
  local copies, waits for them, and re-layouts  6.75 us (2%)
  other arithmetic  3.49 us (1%)
    pallas_call x1, Pallas kernels, norm_and_gather(): pl.pallas_call(functools.partial(norm_kernel, chips_z, kv_count), out_sha...  89.4 us
    pallas_call x1, Pallas kernels, return_sums(): pl.pallas_call(functools.partial(return_kernel, chips_z), out_shape=jax.S...  71.5 us
    pallas_call x1, Pallas kernels, gather_params(): pl.pallas_call(functools.partial(params_kernel, chips_z), out_shape=(jax....  51.5 us
    dot_general x8, matrix products, run_experts(): jnp.dot(grouped[expert], gate_up[piece], preferred_element_type=jnp.float32)  15.1 us
    dot_general x8, matrix products, run_experts(): out = jnp.dot(hidden, down[piece], preferred_element_type=jnp.float32)  7.38 us
  transfers between devices with their start and end apart: 2, of which 0 were waited for; matrix products, arithmetic and copies ran while one was open for 13% of the time, Pallas kernels for 51%

profile of v2, /device:TPU:6, one launch (start us, length us, event | category | flops | bytes accessed | tf_op | source)
XLA Modules:
  0.0 276.9 jit_solution(2012185614369656906)
XLA Ops:
  6.5 0.7 all-gather.3.cloned.1.call-update
  7.3 0.7 all-gather.5.cloned.1.call-update
  10.0 51.5 %shard_map.136 = (bf16[2,4,16,12,384]{4,3,2,1,0:T(8,128)(2,1)}, f32[16,12,128]{2,1,0:T(8,128)}) custom-call(bf16[12,384]{1,0:T(8,128)(2,1)} %bitcast.147, f32[12,128]{1,0:T(8,128)} %pad_maximum_fusion.8.table_ref), custom_call_target="tpu_custom_call" | custom-call | tf_op jit(solution)/shard_map/pallas_call | solution.py:179
  61.5 0.9 fusion.111
  64.2 1.7 copy.42
  67.8 1.7 fusion.114
  72.3 0.7 fusion.45
  73.0 0.7 fusion.44
  73.7 0.7 fusion.43
  74.4 2.3 convolution_convert_fusion
  76.7 89.4 %shard_map.137 = (f32[128,1536]{1,0:T(8,128)}, bf16[16,128,1536]{2,1,0:T(8,128)(2,1)}) custom-call(bf16[4,128,1536]{2,1,0:T(8,128)(2,1)} %bitcast.132, bf16[128,1536]{1,0:T(8,128)(2,1)} %bitcast.145, f32[1,1536]{1,0:T(1,128)} %broadcast_in_dim.34.gain_ref), custom_call_target="tpu_custom_call" | custom-call | tf_op jit(solution)/shard_map/pallas_call | solution.py:268
  166.1 3.8 %fusion.11 = bf16[4,16,16,1536]{3,2,0,1:T(8,128)(2,1)S(1)} fusion(bf16[16,128,1536]{2,1,0:T(8,128)(2,1)} %get-tuple-element.11, f32[16,4,128]{2,1,0:T(4,128)S(1)} %copy.41, f32[16]{0:T(128)S(1)} %iota_convert_fusion, pred[16,4,128]{2,1,0:T(4,128)(4,1)S(1)} %copy.40), kind=kOutput, calls=%fused_computation.13 | convolution fusion | flops 404488192 | bytes 9478208 | tf_op jit(solution)/shard_map/bect,btd->ebcd/dot_general | solution.py:81
  170.3 2.9 %fusion.39 = f32[256,512]{1,0:T(8,128)} fusion(bf16[256,1536]{1,0:T(8,128)(2,1)S(1)} %bitcast.139, bf16[8,1536,512]{2,1,0:T(8,128)(2,1)} %all-gather.3.cloned.1.call-done), kind=kOutput, calls=%fused_computation.59 | convolution fusion | flops 402653184 | bytes 2883584 | tf_op jit(solution)/shard_map/dot_general | solution.py:91
  173.2 3.5 %fusion.38 = f32[256,512]{1,0:T(8,128)} fusion(bf16[256,1536]{1,0:T(8,128)(2,1)S(1)} %bitcast.140, bf16[8,1536,512]{2,1,0:T(8,128)(2,1)} %all-gather.3.cloned.1.call-done), kind=kOutput, calls=%fused_computation.57 | convolution fusion | flops 402653184 | bytes 2883584 | tf_op jit(solution)/shard_map/dot_general | solution.py:91
  176.7 2.8 %fusion.37 = f32[256,512]{1,0:T(8,128)} fusion(bf16[256,1536]{1,0:T(8,128)(2,1)S(1)} %bitcast.137, bf16[8,1536,512]{2,1,0:T(8,128)(2,1)} %all-gather.3.cloned.1.call-done), kind=kOutput, calls=%fused_computation.55 | convolution fusion | flops 402653184 | bytes 2883584 | tf_op jit(solution)/shard_map/dot_general | solution.py:91
  179.5 2.0 fusion.36
  181.5 1.4 fusion.35
  183.4 1.4 fusion.33
  185.4 1.7 fusion.49
  187.1 2.1 fusion.48
  189.3 1.6 fusion.47
  192.9 3.9 %bitcast_convert_fusion.sums_ref = bf16[16,128,1536]{2,1,0:T(8,128)(2,1)} fusion(bf16[16,1,16,1536]{3,2,1,0:T(8,128)(2,1)S(1)} %bitcast.144, bf16[16,1,16,1536]{3,2,1,0:T(8,128)(2,1)S(1)} %bitcast.143, bf16[16,1,16,1536]{3,2,1,0:T(8,128)(2,1)S(1)} %bitcast.142, bf16[16,1,16,1536]{3,2,1,0:T(8,128)(2,1)S(1)} %bitcast.141, f32[16,4,128]{2,1,0:T(4,128)S(1)} %copy.41, ...), kind=kOutput, calls=%fused_computation | convolution fusion | flops 410779648 | bytes 9478208 | tf_op jit(solution)/shard_map/bect,becd->btd/dot_general | solution.py:98
  196.8 71.5 %shard_map.138 = bf16[128,1536]{1,0:T(8,128)(2,1)} custom-call(bf16[16,128,1536]{2,1,0:T(8,128)(2,1)} %bitcast_convert_fusion.sums_ref, f32[128,1536]{1,0:T(8,128)} %get-tuple-element.12.residual_ref), custom_call_target="tpu_custom_call" | custom-call | tf_op jit(solution)/shard_map/pallas_call | solution.py:326
  268.3 1.8 copy.64
  (65 shorter events, 10.5 us)
Async XLA Ops:
  6.5 163.7 %all-gather.3.cloned.1.call-start = ((), (), s32[]{:S(2)}) async-start(), calls=%async_computation | async-start | bytes 14155776 | tf_op jit(solution)/shard_map/all_gather | solution.py:365
  7.3 178.1 %all-gather.5.cloned.1.call-start = ((), (), s32[]{:S(2)}) async-start(), calls=%async_computation.1 | async-start | bytes 7077888 | tf_op jit(solution)/shard_map/all_gather | solution.py:366
  62.5 3.7 %copy-start.5 = (f32[1536]{0:T(1024)S(1)}, f32[1536]{0:T(1024)}, u32[]{:S(2)}) copy-start(f32[1536]{0:T(1024)} %param.23) | copy-start | bytes 18436
  64.1 3.6 %copy-start.7 = (bf16[1,512,384]{2,1,0:T(8,128)(2,1)S(1)}, bf16[1,512,384]{2,1,0:T(8,128)(2,1)}, u32[]{:S(2)}) copy-start(bf16[1,512,384]{2,1,0:T(8,128)(2,1)} %param.15) | copy-start | bytes 1179652
  64.2 3.6 %copy-start.10 = (bf16[1,512,128]{2,1,0:T(8,128)(2,1)S(1)}, bf16[1,512,128]{2,1,0:T(8,128)(2,1)}, u32[]{:S(2)}) copy-start(bf16[1,512,128]{2,1,0:T(8,128)(2,1)} %param.16) | copy-start | bytes 393220
  67.8 2.2 copy-start.8
  71.1 1.2 copy-start.9
  71.1 1.2 copy-start.11
  170.2 11.2 %copy-start.6 = (bf16[8,1536,512]{2,1,0:T(8,128)(2,1)S(1)}, bf16[8,1536,512]{2,1,0:T(8,128)(2,1)}, u32[]{:S(2)}) copy-start(bf16[8,1536,512]{2,1,0:T(8,128)(2,1)} %all-gather.3.cloned.1.call-done) | copy-start | bytes 37748740
  183.4 2.0 copy-start.2
  185.4 3.9 %copy-start.3 = (f32[256,512]{1,0:T(8,128)S(1)}, f32[256,512]{1,0:T(8,128)}, u32[]{:S(2)}) copy-start(f32[256,512]{1,0:T(8,128)} %fusion.35) | copy-start | bytes 1572868
  185.4 5.4 %copy-start = (bf16[8,256,1536]{2,1,0:T(8,128)(2,1)S(1)}, bf16[8,256,1536]{2,1,0:T(8,128)(2,1)}, u32[]{:S(2)}) copy-start(bf16[8,256,1536]{2,1,0:T(8,128)(2,1)} %all-gather.5.cloned.1.call-done) | copy-start | bytes 18874372
  187.1 3.8 %copy-start.4 = (f32[256,512]{1,0:T(8,128)S(1)}, f32[256,512]{1,0:T(8,128)}, u32[]{:S(2)}) copy-start(f32[256,512]{1,0:T(8,128)} %fusion.33) | copy-start | bytes 1572868
  189.3 2.0 copy-start.1
Sparse Core Ops, SparseCore 0:
  9.5 87.7 all-gather.2
  99.4 44.5 all-gather.4
